TPU v7x, 256 devices: a whole 4x4x8 slice. The times are simulated.
256 devices in a mesh: slab: 64 (over y, z, core), grp: 4 (over x).
Axes of the slice: x: 4, y: 4, z: 8, core: 2. Of those that a mesh axis runs over, the one named last changes fastest.
Arguments:
- blocks: bfloat16 [4, 4, 1024, 128, 128], P('grp', None, 'slab'), may hold values from -6 to 6
- coords: int32 [4, 64, 4, 2], P('grp', 'slab'), may hold values from 0 to 15
- counts: int32 [4, 64], P('grp', 'slab'), may hold values from 1 to 4, as said below
- omega1: bfloat16 [1024, 512], replicated, may hold values from -0.1875 to 0.1875
- omega2: bfloat16 [2048, 512], replicated, may hold values from -0.5 to 0.5
- omega3: bfloat16 [2048, 512], replicated, may hold values from -0.125 to 0.125
Outputs:
- core_sketch: float32 [512, 512, 512], P(None, 'slab', 'grp')
Inputs may be any that keep to these rules, and one draw needn't show every extreme that they name: counts[g, s] slots are live in the list of group g on slab s; slots from it on are ignored. Some list holds 4 live slots in every draw.
All inputs are finite; a program needn't handle non-finite values.
Results may differ from a plain program's by a relative error of at most 0.0041.
Values may be sent and summed in bfloat16 or wider, within the bound.
No kernel may reach another device: no remote copies, remote signals or barrier semaphores. Data moves between devices by JAX's collectives and lax.ppermute only.
A program may use at most 128 MiB of HBM per device.

v0:
```python
import jax
import jax.numpy as jnp
from jax import lax
from jax.sharding import PartitionSpec as P


def contract(running, one_block, coordinate, omega2, third_cols):
    block_edge = one_block.shape[-1]
    third_rows = lax.dynamic_slice_in_dim(third_cols, coordinate[1] * block_edge, block_edge, 0)
    second_rows = lax.dynamic_slice_in_dim(omega2, coordinate[0] * block_edge, block_edge, 0)
    after_third = jnp.einsum(
        "iab,bs->ias", one_block, third_rows, preferred_element_type=jnp.float32
    ).astype(jnp.bfloat16)
    return running + jnp.einsum(
        "ias,ar->sir", after_third, second_rows, preferred_element_type=jnp.float32
    )


def local(blocks, coords, counts, omega1, omega2, omega3):
    own_blocks = blocks[0]
    places = coords[0, 0]
    live_count = counts[0, 0]
    slab_depth = own_blocks.shape[1]
    sketch_width = omega2.shape[1]
    empty_sketch = jnp.zeros((omega3.shape[1], slab_depth, sketch_width), jnp.float32)

    def own_step(position, running):
        return contract(running, own_blocks[position], places[position], omega2, omega3)

    sketch = lax.fori_loop(0, live_count, own_step, empty_sketch)
    reduced = lax.psum_scatter(sketch, "grp", scatter_dimension=0, tiled=True).astype(jnp.bfloat16)
    folded = lax.all_to_all(reduced, "slab", split_axis=2, concat_axis=1, tiled=True)
    return jnp.einsum("ir,sip->rps", omega1, folded, preferred_element_type=jnp.float32)


def solution(mesh):
    in_specs = (
        P("grp", None, "slab", None, None),
        P("grp", "slab", None, None),
        P("grp", "slab"),
        P(),
        P(),
        P(),
    )
    out_specs = P(None, "slab", "grp")
    return jax.shard_map(local, mesh=mesh, in_specs=in_specs, out_specs=out_specs, check_vma=False)
```

profile of v0, /device:TPU:1, one launch (start us, length us, event | category | flops | bytes accessed | tf_op | source)
XLA Modules:
  0.0 328.9 jit_solution(5539492059994773851)
XLA Ops:
  6.5 0.0 copy-start
  6.5 0.0 reduce-scatter.2.cloned.1.call-start
  6.5 0.0 copy-start.1
  6.5 7.9 %broadcast_in_dim.3 = f32[512,16,512]{0,2,1:T(8,128)} broadcast(f32[]{:T(128)} %constant.15.clone.1), dimensions={} | broadcast | bytes 16777220 | tf_op jit(solution)/shard_map/broadcast_in_dim | solution.py:25
  14.4 0.0 copy-done.1
  14.4 17.8 %while.10 = (s32[]{:T(128)}, f32[512,16,512]{0,2,1:T(8,128)}, s32[]{:T(128)}, s32[4,2]{0,1:T(2,128)S(1)}, bf16[2048,512]{1,0:T(8,128)(2,1)}, /*index=5*/bf16[4,1...) while((s32[]{:T(128)}, f32[512,16,512]{0,2,1:T(8,128)}, ...), condition=%wide.region_1.0_spmd, body=%wide.region_0.0_spmd.sunk | while | flops 1347420160 | bytes 34341160 | solution.py:30
  15.1 0.1 constant_dynamic-slice_fusion.2
  15.1 0.5 fusion.31
  16.9 14.6 %bitcast_add_fusion.2 = f32[512,16,512]{0,2,1:T(8,128)} fusion(f32[512,16,512]{0,2,1:T(8,128)} %get-tuple-element.149, bf16[4,16,128,128]{3,2,1,0:T(8,128)(2,1)} %get-tuple-element.165, s32[]{:T(128)S(6)} %select_n.13, bf16[2048,512]{1,0:T(8,128)(2,1)} %get-tuple-element.166, s32[]{:T(128)S(6)} %select_n.14, bf16[2048,512]{1,0:T(8,128)(2,1)} %get-tuple-element.164, ...), kind=kOutput, calls=%fused_computation.clone.1 | convolution fusion | flops 1347420160 | bytes 34340876 | tf_op jit(solution)/shard_map/while/body/ias,ar->sir/dot_general | solution.py:14
  32.2 17.7 %copy.18 = f32[512,16,512]{0,1,2:T(8,128)} copy(f32[512,16,512]{0,2,1:T(8,128)} %get-tuple-element.43) | data formatting | bytes 33554432 | tf_op jit(solution)/shard_map/while | solution.py:30
  49.9 0.0 reduce-scatter.2.cloned.1.call-update
  49.9 204.3 %reduce-scatter.2.cloned.1.call-done = f32[128,16,512]{0,1,2:T(8,128)} async-done(((f32[512,16,512]{0,1,2:T(8,128)}), f32[128,16,512]{0,1,2:T(8,128)}) %reduce-scatter.2.cloned.1.call-update) | async-done | bytes 4194320 | tf_op jit(solution)/shard_map/reduce_scatter | solution.py:31
  254.2 2.5 convert_element_type.6
  256.6 61.7 %all_to_all.18 = bf16[128,16,512]{0,1,2:T(8,128)(2,1)S(1)} all-to-all(bf16[128,16,512]{0,1,2:T(8,128)(2,1)S(1)} %convert_element_type.6), channel_id=1, replica_groups=mesh['slab'=64,'grp'=4] {'slab'}, dimensions={2} | all-to-all | bytes 4194304 | tf_op jit(solution)/shard_map/all_to_all | solution.py:32
  318.4 0.5 copy.20
  318.9 0.0 copy-done
  318.9 1.3 fusion.17
  320.2 1.8 copy.22
Async XLA Ops:
  6.5 312.4 %copy-start = (bf16[1024,512]{1,0:T(8,128)(2,1)S(1)}, bf16[1024,512]{1,0:T(8,128)(2,1)}, u32[]{:S(2)}) copy-start(bf16[1024,512]{1,0:T(8,128)(2,1)} %param.11) | copy-start | bytes 3145732
  6.5 247.6 %reduce-scatter.2.cloned.1.call-start = ((), (), s32[]{:S(2)}) async-start(), calls=%async_computation.2 | async-start | bytes 20971520 | tf_op jit(solution)/shard_map/reduce_scatter | solution.py:31
  6.5 7.9 %copy-start.1 = (s32[1,1,4,2]{2,3,1,0:T(2,128)S(1)}, s32[1,1,4,2]{2,3,1,0:T(2,128)}, u32[]{:S(2)}) copy-start(s32[1,1,4,2]{2,3,1,0:T(2,128)} %param.9) | copy-start | bytes 100
Sparse Core Ops, SparseCore 0:
  50.0 204.1 reduce-scatter.1
where the time goes:
time: 329 us
  waiting for transfers between devices  204 us (62%)
  blocking collectives  61.7 us (19%)
  local copies, waits for them, and re-layouts  28.5 us (9%)
  matrix products  15.9 us (5%)
  between operations  13.4 us (4%)
    reduce_scatter x1, waiting for transfers between devices, local(): lax.psum_scatter(sketch, 'grp', scatter_dimension=0, tiled=True)  204 us
    all_to_all x1, blocking collectives, local(): lax.all_to_all(reduced, 'slab', split_axis=2, concat_axis=1, tiled=True)  61.7 us
    while x1, local copies, waits for them, and re-layouts, local(): sketch = lax.fori_loop(0, live_count, own_step, empty_sketch)  17.7 us
    dot_general x1, matrix products, contract(): jnp.einsum('ias,ar->sir', after_third, second_rows, preferred_element_typ...  14.6 us
    broadcast_in_dim x1, local copies, waits for them, and re-layouts, local(): jnp.zeros((omega3.shape[1], slab_depth, sketch_width), jnp.float32)  7.86 us
  transfers between devices with their start and end apart: 1, of which 1 were waited for; matrix products, arithmetic and copies ran while one was open for 0% of the time, Pallas kernels for 0%

commit v1 on v0

--- a/solution.py
+++ b/solution.py
@@ -17,6 +17,15 @@
 
 
 def local(blocks, coords, counts, omega1, omega2, omega3):
+
+    def produce_array_for(state, comm_axis):
+        return jnp.concatenate(
+            jax.lax.all_to_all(
+                jnp.stack(jnp.split(state, jax.lax.axis_size(comm_axis), 2)), comm_axis, 0, 0
+            ),
+            1,
+        )
+
     own_blocks = blocks[0]
     places = coords[0, 0]
     live_count = counts[0, 0]
@@ -29,7 +38,7 @@
 
     sketch = lax.fori_loop(0, live_count, own_step, empty_sketch)
     reduced = lax.psum_scatter(sketch, "grp", scatter_dimension=0, tiled=True).astype(jnp.bfloat16)
-    folded = lax.all_to_all(reduced, "slab", split_axis=2, concat_axis=1, tiled=True)
+    folded = produce_array_for(reduced, "slab")
     return jnp.einsum("ir,sip->rps", omega1, folded, preferred_element_type=jnp.float32)
 
 

time: 329 us -> 313 us (0.951)
  local copies, waits for them, and re-layouts: 28.5 us -> 11.6 us
    while x1 -> x0, local copies, waits for them, and re-layouts: 17.7 us -> none  [local(): sketch = lax.fori_loop(0, live_count, own_step, empty_sketch)]
where the time goes in v1:
time: 313 us
  waiting for transfers between devices  205 us (65%)
  blocking collectives  61.7 us (20%)
  matrix products  15.9 us (5%)
  between operations  13.7 us (4%)
  local copies, waits for them, and re-layouts  11.6 us (4%)
    reduce_scatter x1, waiting for transfers between devices, local(): lax.psum_scatter(sketch, 'grp', scatter_dimension=0, tiled=True)  205 us
    all_to_all x1, blocking collectives, produce_array_for(): jax.lax.all_to_all(jnp.stack(jnp.split(state, jax.lax.axis_size(comm_axis...  61.7 us
    dot_general x1, matrix products, contract(): jnp.einsum('ias,ar->sir', after_third, second_rows, preferred_element_typ...  14.7 us
    broadcast_in_dim x1, local copies, waits for them, and re-layouts, local(): jnp.zeros((omega3.shape[1], slab_depth, sketch_width), jnp.float32)  7.87 us
  transfers between devices with their start and end apart: 1, of which 1 were waited for; matrix products, arithmetic and copies ran while one was open for 0% of the time, Pallas kernels for 0%

profile of v1, /device:TPU:1, one launch (start us, length us, event | category | flops | bytes accessed | tf_op | source)
XLA Modules:
  0.0 313.1 jit_solution(9054220355044883338)
XLA Ops:
  6.5 0.0 copy-start
  6.5 0.0 reduce-scatter.2.cloned.1.call-start
  6.5 0.0 copy-start.1
  6.5 7.9 %broadcast_in_dim.3 = f32[512,16,512]{0,2,1:T(8,128)} broadcast(f32[]{:T(128)} %constant.15.clone.1), dimensions={} | broadcast | bytes 16777220 | tf_op jit(solution)/shard_map/broadcast_in_dim | solution.py:34
  14.4 0.0 copy-done.1
  14.4 18.0 %while.10 = (s32[]{:T(128)}, f32[512,16,512]{0,2,1:T(8,128)}, s32[]{:T(128)}, s32[4,2]{0,1:T(2,128)S(1)}, bf16[2048,512]{1,0:T(8,128)(2,1)}, /*index=5*/bf16[4,1...) while((s32[]{:T(128)}, f32[512,16,512]{0,2,1:T(8,128)}, ...), condition=%wide.region_1.0_spmd, body=%wide.region_0.0_spmd.sunk | while | flops 1347420160 | bytes 34341160 | solution.py:39
  15.1 0.1 constant_dynamic-slice_fusion.2
  15.2 0.6 fusion.31
  17.1 14.7 %bitcast_add_fusion.2 = f32[512,16,512]{0,2,1:T(8,128)} fusion(f32[512,16,512]{0,2,1:T(8,128)} %get-tuple-element.135, bf16[4,16,128,128]{3,2,1,0:T(8,128)(2,1)} %get-tuple-element.151, s32[]{:T(128)S(6)} %select_n.13, bf16[2048,512]{1,0:T(8,128)(2,1)} %get-tuple-element.152, s32[]{:T(128)S(6)} %select_n.14, bf16[2048,512]{1,0:T(8,128)(2,1)} %get-tuple-element.150, ...), kind=kOutput, calls=%fused_computation.clone.1 | convolution fusion | flops 1347420160 | bytes 34340876 | tf_op jit(solution)/shard_map/while/body/ias,ar->sir/dot_general | solution.py:14
  32.4 0.0 reduce-scatter.2.cloned.1.call-update
  32.4 204.9 %reduce-scatter.2.cloned.1.call-done = f32[128,16,512]{0,2,1:T(8,128)} async-done(((f32[512,16,512]{0,2,1:T(8,128)}), f32[128,16,512]{0,2,1:T(8,128)}) %reduce-scatter.2.cloned.1.call-update) | async-done | bytes 4194320 | tf_op jit(solution)/shard_map/reduce_scatter | solution.py:40
  237.3 2.6 convert_element_type.6
  241.4 61.7 %all_to_all.5 = bf16[64,128,16,8]{1,3,2,0:T(8,128)(2,1)S(1)} all-to-all(bf16[64,128,16,8]{1,3,2,0:T(8,128)(2,1)S(1)} %constant_dynamic-update-slice_fusion), channel_id=1, replica_groups=mesh['slab'=64,'grp'=4] {'slab'}, dimensions={0} | all-to-all | bytes 4194304 | tf_op jit(solution)/shard_map/all_to_all | solution.py:23
  303.1 0.0 copy-done
  303.1 1.3 fusion.17
  304.4 1.8 copy.12
  (64 shorter events, 1.2 us)
Async XLA Ops:
  6.5 296.6 %copy-start = (bf16[1024,512]{1,0:T(8,128)(2,1)S(1)}, bf16[1024,512]{1,0:T(8,128)(2,1)}, u32[]{:S(2)}) copy-start(bf16[1024,512]{1,0:T(8,128)(2,1)} %param.11) | copy-start | bytes 3145732
  6.5 230.7 %reduce-scatter.2.cloned.1.call-start = ((), (), s32[]{:S(2)}) async-start(), calls=%async_computation.2 | async-start | bytes 20971520 | tf_op jit(solution)/shard_map/reduce_scatter | solution.py:40
  6.5 7.9 %copy-start.1 = (s32[1,1,4,2]{2,3,1,0:T(2,128)S(1)}, s32[1,1,4,2]{2,3,1,0:T(2,128)}, u32[]{:S(2)}) copy-start(s32[1,1,4,2]{2,3,1,0:T(2,128)} %param.9) | copy-start | bytes 100
Sparse Core Ops, SparseCore 0:
  32.5 204.6 reduce-scatter.1
